TPU v7x, 128 devices: a whole 4x4x4 slice. The times are simulated.
128 devices in a mesh: px: 8 (over z, core), pz: 16 (over x, y).
Axes of the slice: x: 4, y: 4, z: 4, core: 2. Of those that a mesh axis runs over, the one named last changes fastest.
Arguments:
- charge: float32 [32768, 128], P(('px', 'pz')), may hold values from -6 to 6
- dest: int32 [32768, 1], P(('px', 'pz')), may hold values from 0 to 127; in each aligned block of 256 rows (0 to 255, 256 to 511, ...) at most 4 rows name the same one
- local_ids: int32 [32768], P(('px', 'pz')), may hold values from 0 to 255
- green_hat: float32 [128, 128, 2048], P(None, 'px', 'pz'), may hold values from 0.1 to 10, as said below
Outputs:
- potential: float32 [32768, 128], P(('px', 'pz'))
Inputs may be any that keep to these rules, and one draw needn't show every extreme that they name: `dest`: among the 256 slots of one box, no pencil is named by more than 4; some pencil is named by exactly 4. green_hat is even in every dimension: its value at frequencies (k1, k2, k3) equals that at ((128 - k1) mod 2 * 64, (128 - k2) mod 2 * 64, (2048 - k3) mod 2 * 1024) taken in any single dimension.
All inputs are finite; a program needn't handle non-finite values.
Results may differ from a plain program's by a relative error of at most 0.00007.
Values sent between devices are 32-bit elements; how exact they have to be, the bound alone decides.
No kernel may reach another device: no remote copies, remote signals or barrier semaphores. Data moves between devices by JAX's collectives and lax.ppermute only.
A program may use at most 64 MiB of HBM per device.

v0:
```python
import math
import jax
import jax.numpy as jnp
from jax import lax
from jax.sharding import PartitionSpec as P

CXP = 8
CYP = 4
NZP = 1024


def dft_table(n_in, n_out, period, sign):
    rows = lax.broadcasted_iota(jnp.int32, (n_in, n_out), 0)
    cols = lax.broadcasted_iota(jnp.int32, (n_in, n_out), 1)
    phase = (rows * cols % period).astype(jnp.float32) * (2.0 * math.pi / period)
    return (jnp.cos(phase), sign * jnp.sin(phase))


def rotate(real_part, imag_part, cosine, sine, form):
    first = jnp.einsum(form, real_part, cosine, precision=lax.Precision.HIGHEST)
    second = jnp.einsum(form, imag_part, sine, precision=lax.Precision.HIGHEST)
    third = jnp.einsum(form, imag_part, cosine, precision=lax.Precision.HIGHEST)
    fourth = jnp.einsum(form, real_part, sine, precision=lax.Precision.HIGHEST)
    return (first - second, third + fourth)


def solve_field(field, green_hat, wide_x, wide_y):
    cosine, sine = dft_table(NZP, 2 * NZP, 2 * NZP, -1.0)
    real_part = jnp.einsum("xyz,zk->xyk", field, cosine, precision=lax.Precision.HIGHEST)
    imag_part = jnp.einsum("xyz,zk->xyk", field, sine, precision=lax.Precision.HIGHEST)
    turned = lax.all_to_all(
        jnp.stack((real_part, imag_part)), "pz", split_axis=3, concat_axis=2, tiled=True
    )
    cosine, sine = dft_table(wide_y, 2 * wide_y, 2 * wide_y, -1.0)
    real_part, imag_part = rotate(turned[0], turned[1], cosine, sine, "xyk,yq->xqk")
    turned = lax.all_to_all(
        jnp.stack((real_part, imag_part)), "px", split_axis=2, concat_axis=1, tiled=True
    )
    cosine, sine = dft_table(wide_x, 2 * wide_x, 2 * wide_x, -1.0)
    real_part, imag_part = rotate(turned[0], turned[1], cosine, sine, "xyk,xq->qyk")
    real_part = real_part * green_hat
    imag_part = imag_part * green_hat
    cosine, sine = dft_table(2 * wide_x, wide_x, 2 * wide_x, 1.0)
    real_part, imag_part = rotate(real_part, imag_part, cosine, sine, "qyk,qx->xyk")
    turned = lax.all_to_all(
        jnp.stack((real_part, imag_part)), "px", split_axis=1, concat_axis=2, tiled=True
    )
    cosine, sine = dft_table(2 * wide_y, wide_y, 2 * wide_y, 1.0)
    real_part, imag_part = rotate(turned[0], turned[1], cosine, sine, "xqk,qy->xyk")
    turned = lax.all_to_all(
        jnp.stack((real_part, imag_part)), "pz", split_axis=2, concat_axis=3, tiled=True
    )
    cosine, sine = dft_table(2 * NZP, NZP, 2 * NZP, 1.0)
    result = jnp.einsum("xyk,kz->xyz", turned[0], cosine, precision=lax.Precision.HIGHEST)
    result = result - jnp.einsum("xyk,kz->xyz", turned[1], sine, precision=lax.Precision.HIGHEST)
    return result * (1.0 / (8.0 * wide_x * wide_y * NZP))


def local(charge, dest, local_ids, green_hat):
    n_dev = lax.axis_size(("px", "pz"))
    wide_x = CXP * lax.axis_size("px")
    wide_y = CYP * lax.axis_size("pz")
    pencil_blocks = CXP * CYP * NZP // 128
    route = dest[:, 0]
    dense = (
        jnp.zeros((n_dev * pencil_blocks, 128), jnp.float32)
        .at[route * pencil_blocks + local_ids]
        .add(charge)
    )
    pencil = lax.psum_scatter(dense, ("px", "pz"), scatter_dimension=0, tiled=True)
    field = pencil.reshape(CXP, CYP, NZP)
    phi = solve_field(field, green_hat, wide_x, wide_y)
    phi_blocks = phi.reshape(pencil_blocks, 128)
    whole = lax.all_gather(phi_blocks, ("px", "pz"), axis=0, tiled=True)
    return whole[route * pencil_blocks + local_ids]


def solution(mesh):
    return jax.shard_map(
        local,
        mesh=mesh,
        in_specs=(
            P(("px", "pz"), None),
            P(("px", "pz"), None),
            P(("px", "pz")),
            P(None, "px", "pz"),
        ),
        out_specs=P(("px", "pz"), None),
        check_vma=False,
    )
```

profile of v0, /device:TPU:1, one launch (start us, length us, event | category | flops | bytes accessed | tf_op | source)
XLA Modules:
  0.0 1049.4 jit_solution(2361567284407666978)
XLA Ops:
  7.9 8.5 scatter_custom_fusion
  17.0 645.7 %reduce-scatter.2.cloned.1.call-done = f32[256,128]{1,0:T(8,128)} async-done(((f32[32768,128]{1,0:T(8,128)}), f32[256,128]{1,0:T(8,128)}) %reduce-scatter.2.cloned.1.call-update) | async-done | bytes 131088 | tf_op jit(solution)/shard_map/reduce_scatter | solution.py:70
  662.7 0.9 reshape.24
  663.6 35.7 %fusion.32 = f32[1,8,4,2048]{3,1,2,0:T(8,128)S(1)} fusion(f32[8,4,1024]{2,1,0:T(4,128)S(1)} %reshape.24), kind=kOutput, calls=%fused_computation.36 | convolution fusion | flops 834666496 | bytes 393216 | tf_op jit(solution)/shard_map/xyz,zk->xyk/dot_general | solution.py:29
  699.3 36.1 %fusion.35 = f32[1,8,4,2048]{3,1,2,0:T(8,128)S(1)} fusion(f32[8,4,1024]{2,1,0:T(4,128)S(1)} %reshape.24), kind=kOutput, calls=%fused_computation.37 | convolution fusion | flops 836763648 | bytes 393216 | tf_op jit(solution)/shard_map/xyz,zk->xyk/dot_general | solution.py:30
  735.5 5.8 copy.30
  741.3 11.4 %reshape.54 = f32[16,1,8192]{2,1,0:T(1,128)S(1)} reshape(f32[2048,2,4,8]{3,2,1,0:T(4,128)} %bitcast.127) | data formatting | bytes 1048576
  752.7 11.7 %all_to_all.60 = f32[16,1,8192]{2,1,0:T(1,128)S(1)} all-to-all(f32[16,1,8192]{2,1,0:T(1,128)S(1)} %reshape.54), channel_id=1, replica_groups=mesh['px'=8,'pz'=16] {'pz'}, dimensions={0} | all-to-all | bytes 1048576 | tf_op jit(solution)/shard_map/all_to_all | solution.py:31
  765.0 1.9 reduce
  766.9 11.9 %reshape.55 = f32[2048,2,4,8]{3,2,1,0:T(4,128)} reshape(f32[16,8192]{1,0:T(8,128)S(1)} %reduce) | data formatting | bytes 1048576
  778.8 6.7 copy.31
  789.3 51.9 %all_to_all.61 = f32[2,8,128,128]{3,1,0,2:T(8,128)S(1)} all-to-all(f32[2,8,128,128]{3,1,0,2:T(8,128)S(1)} %copy.32), channel_id=1, replica_groups=mesh['px'=8,'pz'=16] {'px'}, dimensions={2} | all-to-all | bytes 2097152 | tf_op jit(solution)/shard_map/all_to_all | solution.py:36
  841.4 1.2 fusion.52
  842.5 1.2 fusion.53
  843.7 1.4 fusion.39
  845.2 0.8 fusion.82
  846.0 1.4 fusion.38
  847.4 0.8 fusion.80
  850.6 18.5 %all_to_all.62 = f32[2,64,16,128]{3,2,0,1:T(8,128)S(1)} all-to-all(f32[2,64,16,128]{3,2,0,1:T(8,128)S(1)} %copy.36), channel_id=1, replica_groups=mesh['px'=8,'pz'=16] {'px'}, dimensions={1} | all-to-all | bytes 2097152 | tf_op jit(solution)/shard_map/all_to_all | solution.py:45
  871.9 12.4 %all_to_all.63 = f32[2,8,64,128]{3,1,0,2:T(8,128)S(1)} all-to-all(f32[2,8,64,128]{3,1,0,2:T(8,128)S(1)} %copy.38), channel_id=1, replica_groups=mesh['px'=8,'pz'=16] {'pz'}, dimensions={2} | all-to-all | bytes 1048576 | tf_op jit(solution)/shard_map/all_to_all | solution.py:50
  884.3 35.3 %fusion.6 = f32[8,4,1024]{2,0,1:T(8,128)S(1)} fusion(f32[2,8,4,16,128]{4,1,3,2,0:T(8,128)S(1)} %bitcast.146), kind=kOutput, calls=%fused_computation.14 | convolution fusion | flops 834666496 | bytes 393216 | tf_op jit(solution)/shard_map/xyk,kz->xyz/dot_general | solution.py:55
  919.6 35.3 %fusion.49 = f32[8,4,1024]{2,0,1:T(8,128)S(1)} fusion(f32[8,4,1024]{2,0,1:T(8,128)S(1)} %fusion.6, f32[2,8,4,16,128]{4,1,3,2,0:T(8,128)S(1)} %bitcast.147), kind=kOutput, calls=%fused_computation.55 | convolution fusion | flops 834732032 | bytes 524288 | tf_op jit(solution)/shard_map/xyk,kz->xyz/dot_general | solution.py:54
  955.7 79.6 %all-gather.2.cloned.1.call-done = f32[32768,128]{1,0:T(8,128)} async-done(((f32[256,128]{1,0:T(8,128)}), f32[32768,128]{1,0:T(8,128)}) %all-gather.2.cloned.1.call-update) | async-done | bytes 16777232 | tf_op jit(solution)/shard_map/all_gather | solution.py:74
  1035.3 7.1 gather_fusion
  (34 shorter events, 12.3 us)
Async XLA Ops:
  6.5 656.2 %reduce-scatter.2.cloned.1.call-start = ((), (), s32[]{:S(2)}) async-start(), calls=%async_computation.5 | async-start | bytes 16908288 | tf_op jit(solution)/shard_map/reduce_scatter | solution.py:70
  16.5 1018.8 %all-gather.2.cloned.1.call-start = ((), (), s32[]{:S(2)}) async-start(), calls=%async_computation.6 | async-start | bytes 16908288 | tf_op jit(solution)/shard_map/all_gather | solution.py:74
  785.5 58.2 %copy-start = (f32[128,16,128]{2,1,0:T(8,128)S(1)}, f32[128,16,128]{2,1,0:T(8,128)}, u32[]{:S(2)}) copy-start(f32[128,16,128]{2,1,0:T(8,128)} %param.7) | copy-start | bytes 3145732
Sparse Core Ops, SparseCore 0:
  16.6 646.0 reduce-scatter.1
  955.8 79.3 all-gather.1
where the time goes:
time: 1050 us
  waiting for transfers between devices  725 us (69%)
  matrix products  156 us (15%)
  blocking collectives  94.5 us (9%)
  local copies, waits for them, and re-layouts  47.1 us (4%)
  between operations  13.9 us (1%)
  other arithmetic  12.1 us (1%)
    reduce_scatter x1, waiting for transfers between devices, local(): lax.psum_scatter(dense, ('px', 'pz'), scatter_dimension=0, tiled=True)  646 us
    all_gather x1, waiting for transfers between devices, local(): whole = lax.all_gather(phi_blocks, ('px', 'pz'), axis=0, tiled=True)  79.6 us
    all_to_all x1, blocking collectives, solve_field(): lax.all_to_all(jnp.stack((real_part, imag_part)), 'px', split_axis=2, con...  51.9 us
    dot_general x1, matrix products, solve_field(): jnp.einsum('xyz,zk->xyk', field, sine, precision=lax.Precision.HIGHEST)  36.1 us
    dot_general x1, matrix products, solve_field(): jnp.einsum('xyz,zk->xyk', field, cosine, precision=lax.Precision.HIGHEST)  35.7 us
    dot_general x1, matrix products, solve_field(): jnp.einsum('xyk,kz->xyz', turned[1], sine, precision=lax.Precision.HIGHEST)  35.3 us
    dot_general x1, matrix products, solve_field(): jnp.einsum('xyk,kz->xyz', turned[0], cosine, precision=lax.Precision.HIGH...  35.3 us
    unnamed x4, local copies, waits for them, and re-layouts  23.3 us
  transfers between devices with their start and end apart: 2, of which 2 were waited for; matrix products, arithmetic and copies ran while one was open for 0% of the time, Pallas kernels for 0%

commit v1 on v0

--- a/solution.py
+++ b/solution.py
@@ -71,7 +71,10 @@
     field = pencil.reshape(CXP, CYP, NZP)
     phi = solve_field(field, green_hat, wide_x, wide_y)
     phi_blocks = phi.reshape(pencil_blocks, 128)
-    whole = lax.all_gather(phi_blocks, ("px", "pz"), axis=0, tiled=True)
+    whole = jnp.concatenate(
+        lax.all_to_all(jnp.stack([phi_blocks] * lax.axis_size(("px", "pz"))), ("px", "pz"), 0, 0),
+        axis=0,
+    )
     return whole[route * pencil_blocks + local_ids]
 
 

time: 1050 us -> 1230 us (1.17)
  waiting for transfers between devices: 725 us -> 887 us
    all_to_all x0 -> x1, waiting for transfers between devices: none -> 241 us  [local(): lax.all_to_all(jnp.stack([phi_blocks] * lax.axis_size(('px', 'pz'))), ('p...]
    all_gather x1 -> x0, waiting for transfers between devices: 79.6 us -> none  [local(): whole = lax.all_gather(phi_blocks, ('px', 'pz'), axis=0, tiled=True)]
where the time goes in v1:
time: 1230 us
  waiting for transfers between devices  887 us (72%)
  matrix products  156 us (13%)
  blocking collectives  94.4 us (8%)
  local copies, waits for them, and re-layouts  54.3 us (4%)
  between operations  13.9 us (1%)
  other arithmetic  12.6 us (1%)
    reduce_scatter x1, waiting for transfers between devices, local(): lax.psum_scatter(dense, ('px', 'pz'), scatter_dimension=0, tiled=True)  646 us
    all_to_all x1, waiting for transfers between devices, local(): lax.all_to_all(jnp.stack([phi_blocks] * lax.axis_size(('px', 'pz'))), ('p...  241 us
    all_to_all x1, blocking collectives, solve_field(): lax.all_to_all(jnp.stack((real_part, imag_part)), 'px', split_axis=2, con...  51.9 us
    dot_general x1, matrix products, solve_field(): jnp.einsum('xyz,zk->xyk', field, sine, precision=lax.Precision.HIGHEST)  36.1 us
    dot_general x1, matrix products, solve_field(): jnp.einsum('xyz,zk->xyk', field, cosine, precision=lax.Precision.HIGHEST)  35.7 us
    dot_general x1, matrix products, solve_field(): jnp.einsum('xyk,kz->xyz', turned[1], sine, precision=lax.Precision.HIGHEST)  35.3 us
    dot_general x1, matrix products, solve_field(): jnp.einsum('xyk,kz->xyz', turned[0], cosine, precision=lax.Precision.HIGH...  35.3 us
  transfers between devices with their start and end apart: 2, of which 2 were waited for; matrix products, arithmetic and copies ran while one was open for 0% of the time, Pallas kernels for 0%

profile of v1, /device:TPU:1, one launch (start us, length us, event | category | flops | bytes accessed | tf_op | source)
XLA Modules:
  0.0 1226.2 jit_solution(5974336737970540642)
XLA Ops:
  7.9 9.0 scatter_custom_fusion
  17.0 646.2 %reduce-scatter.2.cloned.1.call-done = f32[256,128]{1,0:T(8,128)} async-done(((f32[32768,128]{1,0:T(8,128)}), f32[256,128]{1,0:T(8,128)}) %reduce-scatter.2.cloned.1.call-update) | async-done | bytes 131088 | tf_op jit(solution)/shard_map/reduce_scatter | solution.py:70
  663.2 0.9 reshape.26
  664.2 35.7 %fusion.32 = f32[1,8,4,2048]{3,1,2,0:T(8,128)S(1)} fusion(f32[8,4,1024]{2,1,0:T(4,128)S(1)} %reshape.26), kind=kOutput, calls=%fused_computation.36 | convolution fusion | flops 834666496 | bytes 393216 | tf_op jit(solution)/shard_map/xyz,zk->xyk/dot_general | solution.py:29
  699.8 36.1 %fusion.35 = f32[1,8,4,2048]{3,1,2,0:T(8,128)S(1)} fusion(f32[8,4,1024]{2,1,0:T(4,128)S(1)} %reshape.26), kind=kOutput, calls=%fused_computation.37 | convolution fusion | flops 836763648 | bytes 393216 | tf_op jit(solution)/shard_map/xyz,zk->xyk/dot_general | solution.py:30
  736.0 5.8 copy.30
  741.8 11.4 reshape.56
  753.2 11.6 all_to_all.65
  765.3 1.9 reduce
  767.2 11.9 reshape.57
  779.1 6.7 copy.31
  789.7 51.9 %all_to_all.66 = f32[2,8,128,128]{3,1,0,2:T(8,128)S(1)} all-to-all(f32[2,8,128,128]{3,1,0,2:T(8,128)S(1)} %copy.32), channel_id=1, replica_groups=mesh['px'=8,'pz'=16] {'px'}, dimensions={2} | all-to-all | bytes 2097152 | tf_op jit(solution)/shard_map/all_to_all | solution.py:36
  841.7 1.2 fusion.52
  842.9 1.2 fusion.53
  844.1 1.4 fusion.39
  846.3 1.4 fusion.38
  850.9 18.5 %all_to_all.67 = f32[2,64,16,128]{3,2,0,1:T(8,128)S(1)} all-to-all(f32[2,64,16,128]{3,2,0,1:T(8,128)S(1)} %copy.36), channel_id=1, replica_groups=mesh['px'=8,'pz'=16] {'px'}, dimensions={1} | all-to-all | bytes 2097152 | tf_op jit(solution)/shard_map/all_to_all | solution.py:45
  872.2 12.4 %all_to_all.68 = f32[2,8,64,128]{3,1,0,2:T(8,128)S(1)} all-to-all(f32[2,8,64,128]{3,1,0,2:T(8,128)S(1)} %copy.38), channel_id=1, replica_groups=mesh['px'=8,'pz'=16] {'pz'}, dimensions={2} | all-to-all | bytes 1048576 | tf_op jit(solution)/shard_map/all_to_all | solution.py:50
  884.6 35.3 %fusion.6 = f32[8,4,1024]{2,0,1:T(8,128)S(1)} fusion(f32[2,8,4,16,128]{4,1,3,2,0:T(8,128)S(1)} %bitcast.147), kind=kOutput, calls=%fused_computation.14 | convolution fusion | flops 834666496 | bytes 393216 | tf_op jit(solution)/shard_map/xyk,kz->xyz/dot_general | solution.py:55
  919.9 35.3 %fusion.49 = f32[8,4,1024]{2,0,1:T(8,128)S(1)} fusion(f32[8,4,1024]{2,0,1:T(8,128)S(1)} %fusion.6, f32[2,8,4,16,128]{4,1,3,2,0:T(8,128)S(1)} %bitcast.148), kind=kOutput, calls=%fused_computation.55 | convolution fusion | flops 834732032 | bytes 524288 | tf_op jit(solution)/shard_map/xyk,kz->xyz/dot_general | solution.py:54
  955.4 7.8 stack.51
  963.2 8.2 all-to-all-start.4
  971.4 240.7 %all-to-all-done.4 = f32[128,256,128]{2,1,0:T(8,128)} async-done(((f32[128,256,128]{2,1,0:T(8,128)}), f32[128,256,128]{2,1,0:T(8,128)}, u32[]{:S(2)}, u32[]{:S(2)}) %all-to-all-start.4) | async-done | bytes 16777248 | tf_op jit(solution)/shard_map/all_to_all | solution.py:75
  1212.0 7.1 gather_fusion
  (34 shorter events, 12.6 us)
Async XLA Ops:
  6.5 656.7 %reduce-scatter.2.cloned.1.call-start = ((), (), s32[]{:S(2)}) async-start(), calls=%async_computation.6 | async-start | bytes 16908288 | tf_op jit(solution)/shard_map/reduce_scatter | solution.py:70
  785.8 58.2 %copy-start = (f32[128,16,128]{2,1,0:T(8,128)S(1)}, f32[128,16,128]{2,1,0:T(8,128)}, u32[]{:S(2)}) copy-start(f32[128,16,128]{2,1,0:T(8,128)} %param.7) | copy-start | bytes 3145732
  963.2 248.9 %all-to-all-start.4 = ((f32[128,256,128]{2,1,0:T(8,128)}), f32[128,256,128]{2,1,0:T(8,128)}, u32[]{:S(2)}, u32[]{:S(2)}) async-start(f32[128,256,128]{2,1,0:T(8,128)} %stack.51), calls=%async_computation.5 | async-start | bytes 33554432 | tf_op jit(solution)/shard_map/all_to_all | solution.py:75
Sparse Core Ops, SparseCore 0:
  17.1 646.0 reduce-scatter.1
